TPU v7x, 32 devices: a whole 2x2x4 slice. The times are simulated.
32 devices in a mesh: seq: 8 (over z, x), kvh: 2 (over core), batch: 2 (over y).
Axes of the slice: x: 2, y: 2, z: 4, core: 2. Of those that a mesh axis runs over, the one named last changes fastest.
Arguments:
- queries: bfloat16 [8, 512, 3584], P('batch', 'seq', 'kvh'), parts along dimension 0, may hold values from -160 to 160
- text_keys: bfloat16 [8, 512, 512], P('batch', 'seq', 'kvh'), parts along dimension 0, may hold values from -6 to 6
- text_values: bfloat16 [8, 512, 512], P('batch', 'seq', 'kvh'), parts along dimension 0, may hold values from -6 to 6
- visual_keys: bfloat16 [32, 729, 512], P(('batch', 'seq'), None, 'kvh'), parts along dimension 0, may hold values from -6 to 6
- visual_values: bfloat16 [32, 729, 512], P(('batch', 'seq'), None, 'kvh'), parts along dimension 0, may hold values from -6 to 6
- gate_weight: float32 [3584, 28], P('kvh'), may hold values from -0.1875 to 0.1875
- text_offsets: int32 [16], P('batch'), parts along dimension 0, may hold values from 0 to 448, as said below
- image_sequence: int32 [32], P('batch'), parts along dimension 0, may hold values from 0 to 3, as said below
- image_position: int32 [32], P('batch'), parts along dimension 0, may hold values from 0 to 511, as said below
Outputs:
- combined: bfloat16 [8, 512, 3584], P('batch', 'seq', 'kvh'), parts along dimension 0
There are 2 independent parts, one for each index of `batch`. A program takes and returns all parts, laid end to end along the dimension named above; an argument that names none is the same for every part. Nothing has to cross between parts.
Inputs may be any that keep to these rules, and one draw needn't show every extreme that they name: A permutation of the multiples of 64 below 512: text block j holds the positions text_offsets[j] to text_offsets[j] + 63. `image_sequence`: each of the 4 sequences owns exactly 4 images. `image_position`: every sequence has an image at position 0.
All inputs are finite; a program needn't handle non-finite values.
Results may differ from a plain program's by a relative error of at most 0.0039.
Values may be sent and summed in bfloat16 or wider, within the bound.
A program may use at most 128 MiB of HBM per device.

v0:
```python
import jax
import jax.numpy as jnp
from jax import lax
from jax.sharding import PartitionSpec as P

HQ = 28
DH = 128
GROUP = 7


NEG = -1e30


def block_stats(query_rows, key_blocks, value_blocks, visible):
    scaling = 1.0 / query_rows.shape[-1] ** 0.5
    scores = (
        jnp.einsum("tghe,bkge->tghbk", query_rows, key_blocks, preferred_element_type=jnp.float32)
        * scaling
    )
    allowed = visible[:, None, None, :, :]
    scores = jnp.where(allowed, scores, NEG)
    block_peak = jnp.max(scores, axis=-1)
    unnormed = jnp.where(allowed, jnp.exp(scores - block_peak[..., None]), 0.0)
    block_total = jnp.sum(unnormed, axis=-1)
    block_sum = jnp.einsum(
        "tghbk,bkge->tghbe",
        unnormed.astype(jnp.bfloat16),
        value_blocks,
        preferred_element_type=jnp.float32,
    )
    return (block_peak, block_total, block_sum)


def fold_blocks(running, block_peak, block_total, block_sum):
    running_peak, denominator, numerator = running
    new_peak = jnp.maximum(running_peak, jnp.max(block_peak, axis=-1))
    rescale = jnp.exp(running_peak - new_peak)
    weights = jnp.exp(block_peak - new_peak[..., None])
    denominator = jnp.sum(weights * block_total, axis=-1)
    numerator = jnp.sum(weights[..., None] * block_sum, axis=-2)
    return (new_peak, denominator, numerator)


def empty_state(lead_shape, width):
    return (
        jnp.full(lead_shape, NEG, jnp.float32),
        jnp.zeros(lead_shape, jnp.float32),
        jnp.zeros(lead_shape + (width,), jnp.float32),
    )


def on_device(
    queries,
    text_keys,
    text_values,
    visual_keys,
    visual_values,
    gate_weight,
    text_offsets,
    image_sequence,
    image_position,
):
    seqs_here, rows_here, columns = queries.shape
    groups = text_keys.shape[-1] // DH
    shaped = queries.reshape(seqs_here, rows_here, groups, GROUP, DH)
    mine = lax.axis_index("seq")
    row_range = jnp.arange(rows_here, dtype=jnp.int32)
    query_pos = text_offsets[mine] + row_range
    partial_gate = jnp.dot(
        queries.reshape(seqs_here * rows_here, columns).astype(jnp.float32),
        gate_weight,
        precision=lax.Precision.HIGHEST,
    )
    gate_logits = lax.psum_scatter(
        partial_gate.reshape(seqs_here, rows_here, HQ), "kvh", scatter_dimension=2, tiled=True
    )
    gate = jax.nn.sigmoid(gate_logits).reshape(seqs_here, rows_here, groups, GROUP)
    row_lead = (rows_here, groups, GROUP)
    keys_all, values_all = (
        lax.all_gather(text_keys, "seq", axis=1, tiled=True),
        lax.all_gather(text_values, "seq", axis=1, tiled=True),
    )
    block_count = keys_all.shape[1] // rows_here
    key_blocks = keys_all.reshape(seqs_here, block_count, rows_here, groups, DH)
    value_blocks = values_all.reshape(seqs_here, block_count, rows_here, groups, DH)
    key_pos = text_offsets[:, None] + row_range[None, :]
    text_visible = key_pos[None, :, :] <= query_pos[:, None, None]

    def text_one(members):
        query_rows, keys_here, values_here = members
        stats = block_stats(query_rows, keys_here, values_here, text_visible)
        return fold_blocks(empty_state(row_lead, DH), *stats)

    text_state = lax.map(text_one, (shaped, key_blocks, value_blocks))
    vis_tokens = visual_keys.shape[1]
    image_keys, image_values = (
        lax.all_gather(visual_keys, "seq", axis=0, tiled=True),
        lax.all_gather(visual_values, "seq", axis=0, tiled=True),
    )
    per_seq = image_sequence.shape[0] // seqs_here
    order = jnp.argsort(image_sequence, stable=True).reshape(seqs_here, per_seq)
    chosen_keys = image_keys[order].reshape(seqs_here, per_seq, vis_tokens, groups, DH)
    chosen_values = image_values[order].reshape(seqs_here, per_seq, vis_tokens, groups, DH)
    chosen_places = image_position[order]

    def visual_one(members):
        query_rows, keys_here, values_here, places_here = members
        visible = jnp.broadcast_to(
            places_here[None, :, None] <= query_pos[:, None, None], (rows_here, per_seq, vis_tokens)
        )
        stats = block_stats(query_rows, keys_here, values_here, visible)
        return fold_blocks(empty_state(row_lead, DH), *stats)

    visual_state = lax.map(visual_one, (shaped, chosen_keys, chosen_values, chosen_places))
    text_out = text_state[2] / text_state[1][..., None]
    visual_out = visual_state[2] / visual_state[1][..., None]
    mixed = (1.0 - gate)[..., None] * text_out + gate[..., None] * visual_out
    return mixed.astype(jnp.bfloat16).reshape(seqs_here, rows_here, columns)


def solution(mesh):
    return jax.shard_map(
        on_device,
        mesh=mesh,
        in_specs=(
            P("batch", "seq", "kvh"),
            P("batch", "seq", "kvh"),
            P("batch", "seq", "kvh"),
            P(("batch", "seq"), None, "kvh"),
            P(("batch", "seq"), None, "kvh"),
            P("kvh", None),
            P("batch"),
            P("batch"),
            P("batch"),
        ),
        out_specs=P("batch", "seq", "kvh"),
        check_vma=False,
    )
```

profile of v0, /device:TPU:0, one launch (start us, length us, event | category | flops | bytes accessed | tf_op | source)
XLA Modules:
  0.0 372.9 jit_solution(50887487505098522)
XLA Ops:
  17.3 3.9 %all-reduce = f32[4,64,28]{1,0,2:T(4,128)S(1)} all-reduce(f32[4,64,28]{1,0,2:T(4,128)S(1)} %copy.32), channel_id=2, replica_groups=mesh['seq'=8,'kvh'=2,'batch'=2] {'kvh'}, use_global_device_ids=true, to_apply=%region_0.0.clone | all-reduce | flops 7168 | bytes 57344
  23.9 28.7 %all-gather.5.cloned.1.call-done = bf16[4,512,256]{2,1,0:T(8,128)(2,1)} async-done(((bf16[4,64,256]{2,1,0:T(8,128)(2,1)}), bf16[4,512,256]{2,1,0:T(8,128)(2,1)}) %all-gather.5.cloned.1.call-update) | async-done | bytes 1048592 | tf_op jit(solution)/shard_map/all_gather | solution.py:80
  52.6 2.1 reshape.128
  54.8 39.0 %all-gather.7.cloned.1.call-done = bf16[4,512,256]{2,1,0:T(8,128)(2,1)} async-done(((bf16[4,64,256]{2,1,0:T(8,128)(2,1)}), bf16[4,512,256]{2,1,0:T(8,128)(2,1)}) %all-gather.7.cloned.1.call-update) | async-done | bytes 1048592 | tf_op jit(solution)/shard_map/all_gather | solution.py:81
  93.8 2.1 reshape.130
  96.2 25.2 %while.26 = (s32[]{:T(128)}, f32[4,64,2,7]{1,3,2,0:T(8,128)S(1)}, f32[4,64,2,7,128]{4,1,3,2,0:T(8,128)S(1)}, bf16[4,8,64,2,128]{4,3,2,1,0:T(2,128)(2,1)}, bf16[4...) while((s32[]{:T(128)}, f32[4,64,2,7]{1,3,2,0:T(8,128)S(1)}, ...), condition=%wide.region_7.8_spmd.clone, body=%wide.region_1.7_spmd.clone.sunk | while | flops 243062912 | bytes 9113461 | solution.py:94
  100.3 2.1 fusion.64
  106.6 2.1 fusion.64
  112.9 2.1 fusion.64
  119.2 2.1 fusion.64
  121.4 68.9 %all-gather.9.cloned.1.call-done = bf16[16,729,256]{2,1,0:T(8,128)(2,1)} async-done(((bf16[2,729,256]{2,1,0:T(8,128)(2,1)}), bf16[16,729,256]{2,1,0:T(8,128)(2,1)}) %all-gather.9.cloned.1.call-update) | async-done | bytes 5971984 | tf_op jit(solution)/shard_map/all_gather | solution.py:97
  190.2 6.2 %gather_fusion.1 = bf16[16,729,256]{2,1,0:T(8,128)(2,1)} fusion(bf16[16,729,256]{2,1,0:T(8,128)(2,1)} %all-gather.9.cloned.1.call-done, s32[1024]{0:T(1024)S(1)} %pad_clamp_fusion), kind=kCustom, calls=%fused_computation.1 | custom fusion | bytes 11944000 | tf_op jit(solution)/shard_map/gather | solution.py:102
  196.4 8.7 %copy.39 = bf16[16,729,256]{1,2,0:T(8,128)(2,1)} copy(bf16[16,729,256]{2,1,0:T(8,128)(2,1)} %gather_fusion.1) | data formatting | bytes 11943936 | tf_op jit(solution)/shard_map/gather | solution.py:102
  205.1 8.6 %copy.42 = bf16[4,4,729,2,128]{4,2,1,3,0:T(8,128)(2,1)} copy(bf16[4,4,729,2,128]{2,4,3,1,0:T(8,128)(2,1)} %bitcast.135) | data formatting | bytes 11943936
  213.7 72.3 %all-gather.11.cloned.1.call-done = bf16[16,729,256]{2,1,0:T(8,128)(2,1)} async-done(((bf16[2,729,256]{2,1,0:T(8,128)(2,1)}), bf16[16,729,256]{2,1,0:T(8,128)(2,1)}) %all-gather.11.cloned.1.call-update) | async-done | bytes 5971984 | tf_op jit(solution)/shard_map/all_gather | solution.py:98
  286.0 6.2 %gather_fusion.2 = bf16[16,729,256]{2,1,0:T(8,128)(2,1)} fusion(bf16[16,729,256]{2,1,0:T(8,128)(2,1)} %all-gather.11.cloned.1.call-done, s32[1024]{0:T(1024)S(1)} %pad_clamp_fusion), kind=kCustom, calls=%fused_computation.2 | custom fusion | bytes 11944000 | tf_op jit(solution)/shard_map/gather | solution.py:103
  292.2 8.6 %copy.41 = bf16[16,729,256]{1,2,0:T(8,128)(2,1)} copy(bf16[16,729,256]{2,1,0:T(8,128)(2,1)} %gather_fusion.2) | data formatting | bytes 11943936 | tf_op jit(solution)/shard_map/gather | solution.py:103
  300.8 8.5 %copy.44 = bf16[4,4,729,2,128]{4,2,1,3,0:T(8,128)(2,1)} copy(bf16[4,4,729,2,128]{2,4,3,1,0:T(8,128)(2,1)} %bitcast.136) | data formatting | bytes 11943936
  309.5 50.5 %while.27 = (s32[]{:T(128)}, f32[4,64,2,7]{1,3,2,0:T(8,128)S(1)}, f32[4,64,2,7,128]{4,1,3,2,0:T(8,128)S(1)}, s32[4,4]{1,0:T(4,128)S(1)}, bf16[4,4,729,2,128]{4,2...) while((s32[]{:T(128)}, f32[4,64,2,7]{1,3,2,0:T(8,128)S(1)}, ...), condition=%wide.region_15.16_spmd.clone, body=%wide.region_9.15_spmd.clone.sunk | while | flops 1375105024 | bytes 36125096 | solution.py:114
  310.3 3.3 fusion.68
  313.5 4.2 %fusion.69 = (f32[64,2,7,4]{0,2,3,1:T(8,128)S(1)}, f32[64,2,7]{0,2,1:T(8,128)S(1)}) fusion(f32[2,4,729,64,7]{2,3,4,1,0:T(8,128)S(1)} %get-tuple-element.329, f32[64,2,7,4]{0,2,3,1:T(8,128)S(1)} %get-tuple-element.330, pred[64,4]{0,1:T(4,128)(4,1)S(1)} %broadcast_compare_fusion.5), kind=kLoop, calls=%fused_computation.38.clone.1 | loop fusion | flops 15671936 | bytes 10483456 | tf_op jit(solution)/shard_map/while/body/eval_jaxpr/reduce_sum | solution.py:24
  317.8 4.3 %fusion.70 = f32[64,2,7,128]{3,0,2,1:T(8,128)S(1)} fusion(f32[2,4,729,64,7]{2,3,4,1,0:T(8,128)S(1)} %get-tuple-element.329, f32[64,2,7,4]{0,2,3,1:T(8,128)S(1)} %get-tuple-element.330, pred[64,4]{0,1:T(4,128)(4,1)S(1)} %broadcast_compare_fusion.5, bf16[4,4,729,2,128]{4,2,1,3,0:T(8,128)(2,1)} %get-tuple-element.359, s32[]{:T(128)S(6)} %copy.72, ...), kind=kOutput, calls=%fused_computation.44.clone.1 | convolution fusion | flops 682726912 | bytes 12445956 | tf_op jit(solution)/shard_map/while/body/eval_jaxpr/tghbk,bkge->tghbe/dot_general | solution.py:25
  322.9 3.3 fusion.68
  326.2 4.2 %fusion.69 = (f32[64,2,7,4]{0,2,3,1:T(8,128)S(1)}, f32[64,2,7]{0,2,1:T(8,128)S(1)}) fusion(f32[2,4,729,64,7]{2,3,4,1,0:T(8,128)S(1)} %get-tuple-element.329, f32[64,2,7,4]{0,2,3,1:T(8,128)S(1)} %get-tuple-element.330, pred[64,4]{0,1:T(4,128)(4,1)S(1)} %broadcast_compare_fusion.5), kind=kLoop, calls=%fused_computation.38.clone.1 | loop fusion | flops 15671936 | bytes 10483456 | tf_op jit(solution)/shard_map/while/body/eval_jaxpr/reduce_sum | solution.py:24
  330.4 4.3 %fusion.70 = f32[64,2,7,128]{3,0,2,1:T(8,128)S(1)} fusion(f32[2,4,729,64,7]{2,3,4,1,0:T(8,128)S(1)} %get-tuple-element.329, f32[64,2,7,4]{0,2,3,1:T(8,128)S(1)} %get-tuple-element.330, pred[64,4]{0,1:T(4,128)(4,1)S(1)} %broadcast_compare_fusion.5, bf16[4,4,729,2,128]{4,2,1,3,0:T(8,128)(2,1)} %get-tuple-element.359, s32[]{:T(128)S(6)} %copy.72, ...), kind=kOutput, calls=%fused_computation.44.clone.1 | convolution fusion | flops 682726912 | bytes 12445956 | tf_op jit(solution)/shard_map/while/body/eval_jaxpr/tghbk,bkge->tghbe/dot_general | solution.py:25
  335.5 3.3 fusion.68
  338.8 4.2 %fusion.69 = (f32[64,2,7,4]{0,2,3,1:T(8,128)S(1)}, f32[64,2,7]{0,2,1:T(8,128)S(1)}) fusion(f32[2,4,729,64,7]{2,3,4,1,0:T(8,128)S(1)} %get-tuple-element.329, f32[64,2,7,4]{0,2,3,1:T(8,128)S(1)} %get-tuple-element.330, pred[64,4]{0,1:T(4,128)(4,1)S(1)} %broadcast_compare_fusion.5), kind=kLoop, calls=%fused_computation.38.clone.1 | loop fusion | flops 15671936 | bytes 10483456 | tf_op jit(solution)/shard_map/while/body/eval_jaxpr/reduce_sum | solution.py:24
  343.0 4.3 %fusion.70 = f32[64,2,7,128]{3,0,2,1:T(8,128)S(1)} fusion(f32[2,4,729,64,7]{2,3,4,1,0:T(8,128)S(1)} %get-tuple-element.329, f32[64,2,7,4]{0,2,3,1:T(8,128)S(1)} %get-tuple-element.330, pred[64,4]{0,1:T(4,128)(4,1)S(1)} %broadcast_compare_fusion.5, bf16[4,4,729,2,128]{4,2,1,3,0:T(8,128)(2,1)} %get-tuple-element.359, s32[]{:T(128)S(6)} %copy.72, ...), kind=kOutput, calls=%fused_computation.44.clone.1 | convolution fusion | flops 682726912 | bytes 12445956 | tf_op jit(solution)/shard_map/while/body/eval_jaxpr/tghbk,bkge->tghbe/dot_general | solution.py:25
  348.1 3.3 fusion.68
  351.4 4.2 %fusion.69 = (f32[64,2,7,4]{0,2,3,1:T(8,128)S(1)}, f32[64,2,7]{0,2,1:T(8,128)S(1)}) fusion(f32[2,4,729,64,7]{2,3,4,1,0:T(8,128)S(1)} %get-tuple-element.329, f32[64,2,7,4]{0,2,3,1:T(8,128)S(1)} %get-tuple-element.330, pred[64,4]{0,1:T(4,128)(4,1)S(1)} %broadcast_compare_fusion.5), kind=kLoop, calls=%fused_computation.38.clone.1 | loop fusion | flops 15671936 | bytes 10483456 | tf_op jit(solution)/shard_map/while/body/eval_jaxpr/reduce_sum | solution.py:24
  355.6 4.3 %fusion.70 = f32[64,2,7,128]{3,0,2,1:T(8,128)S(1)} fusion(f32[2,4,729,64,7]{2,3,4,1,0:T(8,128)S(1)} %get-tuple-element.329, f32[64,2,7,4]{0,2,3,1:T(8,128)S(1)} %get-tuple-element.330, pred[64,4]{0,1:T(4,128)(4,1)S(1)} %broadcast_compare_fusion.5, bf16[4,4,729,2,128]{4,2,1,3,0:T(8,128)(2,1)} %get-tuple-element.359, s32[]{:T(128)S(6)} %copy.72, ...), kind=kOutput, calls=%fused_computation.44.clone.1 | convolution fusion | flops 682726912 | bytes 12445956 | tf_op jit(solution)/shard_map/while/body/eval_jaxpr/tghbk,bkge->tghbe/dot_general | solution.py:25
  360.0 3.8 %add_convert_fusion = bf16[4,64,2,7,128]{4,1,3,2,0:T(8,128)(2,1)S(1)} fusion(f32[4,64,2,7,128]{4,1,3,2,0:T(8,128)S(1)} %get-tuple-element.90, f32[4,64,2,7,128]{4,1,3,2,0:T(8,128)} %copy-done.3, f32[4,64,2,7]{1,3,2,0:T(8,128)S(1)} %get-tuple-element.91, f32[4,64,2,7]{1,3,2,0:T(8,128)S(1)} %copy.37, f32[4,64,2,7]{1,3,2,0:T(8,128)S(1)} %get-tuple-element.88, ...), kind=kLoop, calls=%fused_computation.66 | loop fusion | flops 2752512 | bytes 4644864 | tf_op jit(solution)/shard_map/convert_element_type | solution.py:118
  (112 shorter events, 35.1 us)
Async XLA Ops:
  6.5 9.4 %copy-start = (f32[1792,28]{0,1:T(8,128)S(1)}, f32[1792,28]{0,1:T(8,128)}, u32[]{:S(2)}) copy-start(f32[1792,28]{0,1:T(8,128)} %param.18) | copy-start | bytes 602116
  6.5 5.8 %copy-start.6 = (s32[16]{0:T(128)S(1)}, s32[16]{0:T(128)}, u32[]{:S(2)}) copy-start(s32[16]{0:T(128)} %param.20) | copy-start | bytes 196
  6.5 7.3 %copy-start.2 = (s32[16]{0:T(128)S(1)}, s32[16]{0:T(128)}, u32[]{:S(2)}) copy-start(s32[16]{0:T(128)} %param.21) | copy-start | bytes 196
  6.5 8.1 %copy-start.4 = (bf16[4,64,1792]{2,1,0:T(8,128)(2,1)S(1)}, bf16[4,64,1792]{2,1,0:T(8,128)(2,1)}, u32[]{:S(2)}) copy-start(bf16[4,64,1792]{2,1,0:T(8,128)(2,1)} %param.13) | copy-start | bytes 2752516
  6.5 46.1 %all-gather.5.cloned.1.call-start = ((), (), s32[]{:S(2)}) async-start(), calls=%async_computation | async-start | bytes 1179648 | tf_op jit(solution)/shard_map/all_gather | solution.py:80
  7.3 86.5 %all-gather.7.cloned.1.call-start = ((), (), s32[]{:S(2)}) async-start(), calls=%async_computation.1 | async-start | bytes 1179648 | tf_op jit(solution)/shard_map/all_gather | solution.py:81
  8.0 182.2 %all-gather.9.cloned.1.call-start = ((), (), s32[]{:S(2)}) async-start(), calls=%async_computation.2 | async-start | bytes 6782976 | tf_op jit(solution)/shard_map/all_gather | solution.py:97
  10.2 275.8 %all-gather.11.cloned.1.call-start = ((), (), s32[]{:S(2)}) async-start(), calls=%async_computation.3 | async-start | bytes 6782976 | tf_op jit(solution)/shard_map/all_gather | solution.py:98
  13.8 7.4 %copy-start.7 = (u32[32]{0:T(128)S(1)}, u32[32]{0:T(128)}, u32[]{:S(2)}) copy-start(u32[32]{0:T(128)} %constant.68) | copy-start | bytes 388
  13.8 8.7 %copy-start.5 = (s32[8]{0:T(128)S(1)}, s32[8]{0:T(128)}, u32[]{:S(2)}) copy-start(s32[8]{0:T(128)} %param.19) | copy-start | bytes 100
  121.4 75.1 %copy-start.3 = (f32[4,64,2,7,128]{4,1,3,2,0:T(8,128)}, f32[4,64,2,7,128]{4,1,3,2,0:T(8,128)S(1)}, u32[]{:S(2)}) copy-start(f32[4,64,2,7,128]{4,1,3,2,0:T(8,128)S(1)} %get-tuple-element.87) | copy-start | bytes 5505028
  360.0 6.3 %copy-start.1 = (f32[1792,28]{0,1:T(8,128)S(1)}, f32[1792,28]{0,1:T(8,128)}, u32[]{:S(2)}) copy-start(f32[1792,28]{0,1:T(8,128)} %param.18) | copy-start | bytes 602116
Sparse Core Ops, SparseCore 0:
  9.5 43.0 all-gather.4
  54.8 38.9 all-gather.6
  96.0 94.1 all-gather.8
  192.3 93.6 all-gather.10
where the time goes:
time: 374 us; the launch traced here: 373 us
  waiting for transfers between devices  210 us (56%)
  local copies, waits for them, and re-layouts  67.9 us (18%)
  matrix products  44 us (12%)
  other arithmetic  32 us (9%)
  between operations  14 us (4%)
  blocking collectives  3.9 us (1%)
    all_gather x1, waiting for transfers between devices, on_device(): lax.all_gather(visual_values, 'seq', axis=0, tiled=True)  72.3 us
    all_gather x1, waiting for transfers between devices, on_device(): lax.all_gather(visual_keys, 'seq', axis=0, tiled=True)  68.9 us
    all_gather x1, waiting for transfers between devices, on_device(): lax.all_gather(text_values, 'seq', axis=1, tiled=True)  39 us
    all_gather x1, waiting for transfers between devices, on_device(): lax.all_gather(text_keys, 'seq', axis=1, tiled=True)  28.7 us
    dot_general x8, matrix products, block_stats(): jnp.einsum('tghbk,bkge->tghbe', unnormed.astype(jnp.bfloat16), value_bloc...  25.8 us
    reduce_sum x8, other arithmetic, block_stats(): block_total = jnp.sum(unnormed, axis=-1)  22.7 us
    unnamed x22, local copies, waits for them, and re-layouts  22.2 us
    dot_general x8, matrix products, block_stats(): jnp.einsum('tghe,bkge->tghbk', query_rows, key_blocks, preferred_element_...  16.8 us
  transfers between devices with their start and end apart: 4, of which 4 were waited for; matrix products, arithmetic and copies ran while one was open for 17% of the time, Pallas kernels for 0%

commit v1 on v0

v1 whole, which is shorter than its diff:
```python
import functools
import math

import jax
import jax.numpy as jnp
from jax import lax
from jax.experimental import pallas as pl
from jax.experimental.pallas import tpu as pltpu
from jax.sharding import PartitionSpec as P

DH = 128
GROUP = 7
LANES = 128
HALF = LANES // 2
NEG = -1e30
FLOOR = -1e29
FAR = 1 << 30
SCALE = 1.0 / DH ** 0.5
SCALE2 = SCALE * math.log2(math.e)


def heads_of(ref, lead, g):
    start = pl.multiple_of(g * (GROUP * DH), DH)
    return jnp.concatenate(
        [ref[lead, :, pl.ds(start + h * DH, DH)] for h in range(GROUP)], axis=0
    )


def put_heads(ref, lead, g, stacked):
    rows = stacked.shape[0] // GROUP
    start = pl.multiple_of(g * (GROUP * DH), DH)
    for h in range(GROUP):
        ref[(*lead, slice(None), pl.ds(start + h * DH, DH))] = stacked[h * rows:(h + 1) * rows]


def pack_stats(peak, total, rows):
    lane = lax.broadcasted_iota(jnp.int32, (rows, LANES), 1)
    packed = jnp.zeros((rows, LANES), jnp.float32)
    for h in range(GROUP):
        here = slice(h * rows, (h + 1) * rows)
        packed = jnp.where(lane == h, peak[here], packed)
        packed = jnp.where(lane == HALF + h, total[here], packed)
    return packed


def totals_of(packed):
    return pltpu.roll(packed, HALF, 1)


def softmax_parts(q, keys, values, bias):
    scores = lax.dot_general(
        q, keys, (((1,), (1,)), ((), ())), preferred_element_type=jnp.float32
    )
    if bias is not None:
        rows, count = bias.shape
        scores = (scores.reshape(GROUP, rows, count) + bias[None]).reshape(GROUP * rows, count)
    peak = jnp.maximum(jnp.max(scores, axis=-1, keepdims=True), FLOOR)
    expd = jnp.exp2((scores - peak) * SCALE2)
    total = jnp.sum(expd, axis=-1, keepdims=True)
    num = jnp.dot(expd.astype(jnp.bfloat16), values, preferred_element_type=jnp.float32)
    return peak * SCALE, total, num


def attention_kernel(
    n, seqs, rows, groups, here, per_seq,
    owners, places, at, thresholds,
    queries, text_keys, text_values, visual_keys, visual_values,
    text_ref, visual_ref,
    q_pair, far_tk, far_tv, far_ik, far_iv, num, stat, cat_k, cat_v,
    t_send, t_stat_send, t_recv, t_stat_recv, v_send, v_stat_send, v_recv, v_stat_recv,
    t_own_stat, send_sems, recv_sems,
):
    me = lax.axis_index("seq")
    members = n // 4
    blocks = n // 2
    pair = me // 4 * 4 + (me + 2) % 4
    side = me // 2 * 2 + (me + 1) % 2
    others = [(me // 4 + k) % members * 4 + me % 4 for k in range(1, members)]

    barrier = pltpu.get_barrier_semaphore()
    for peer in (pair, side, *others):
        pl.semaphore_signal(
            barrier, inc=1, device_id={"seq": peer}, device_id_type=pl.DeviceIdType.MESH
        )
    pl.semaphore_wait(barrier, 2 + len(others))

    copies = []

    def send(src, dst, peer):
        copy = pltpu.make_async_remote_copy(
            src_ref=src,
            dst_ref=dst,
            send_sem=send_sems.at[len(copies)],
            recv_sem=recv_sems.at[len(copies)],
            device_id={"seq": peer},
            device_id_type=pl.DeviceIdType.MESH,
        )
        copy.start()
        copies.append(copy)
        return copy

    def slot_of(kind, k=0):
        return {"side": 0, "far": k, "diag": members - 1 + k}[kind]

    q_copy = send(queries, q_pair, pair)
    text_far = []
    for k, peer in enumerate(others, 1):
        s = slot_of("far", k)
        text_far.append((send(text_keys, far_tk.at[s], peer), send(text_values, far_tv.at[s], peer)))
    text_side = (send(text_keys, far_tk.at[0], side), send(text_values, far_tv.at[0], side))
    image_far = {}
    image_side = {}
    for j in range(here):
        for k, peer in enumerate(others, 1):
            s = slot_of("far", k)
            image_far[k, j] = (
                send(visual_keys.at[j], far_ik.at[s, j], peer),
                send(visual_values.at[j], far_iv.at[s, j], peer),
            )
        image_side[j] = (
            send(visual_keys.at[j], far_ik.at[0, j], side),
            send(visual_values.at[j], far_iv.at[0, j], side),
        )

    def attend(keys, values, index, sides):
        owner = owners[index]

        def step(g, carry):
            at_g = pl.ds(pl.multiple_of(g * DH, DH), DH)
            k, v = keys[:, at_g], values[:, at_g]
            for which in sides:
                q = heads_of(queries if which == 0 else q_pair, owner, g)
                peak, total, out = softmax_parts(q, k, v, None)
                put_heads(num, (index, which), g, out)
                stat[index, which, g] = pack_stats(peak, total, rows)
            return carry

        lax.fori_loop(0, groups, step, 0)

    for j in range(here):
        attend(visual_keys.at[j], visual_values.at[j], j, (0,))

    text_diag = []
    for k, pieces in enumerate(text_far, 1):
        for piece in pieces:
            piece.wait_recv()
        s, d = slot_of("far", k), slot_of("diag", k)
        text_diag.append((
            send(far_tk.at[s], far_tk.at[d], side), send(far_tv.at[s], far_tv.at[d], side)
        ))

    q_copy.wait_recv()
    for j in range(here):
        attend(visual_keys.at[j], visual_values.at[j], j, (1,))

    for piece in (*text_side, *[p for pieces in text_diag for p in pieces]):
        piece.wait_recv()
    for b in range(blocks):
        span = pl.ds(b * rows, rows)
        cat_k[:, span, :] = text_keys[...] if b == 0 else far_tk[b - 1]
        cat_v[:, span, :] = text_values[...] if b == 0 else far_tv[b - 1]
    count = blocks * rows
    lane = lax.broadcasted_iota(jnp.int32, (rows, count), 1)
    row = lax.broadcasted_iota(jnp.int32, (rows, count), 0)
    key_pos = lane % rows
    for b in range(blocks):
        inside = (lane >= b * rows) & (lane < (b + 1) * rows)
        key_pos = key_pos + jnp.where(inside, places[2 + b], 0)
    biases = [jnp.where(key_pos <= row + places[which], 0.0, NEG) for which in (0, 1)]

    def text_step(i, carry):
        s, g = i // groups, i % groups
        at_g = pl.ds(pl.multiple_of(g * DH, DH), DH)
        k, v = cat_k[s, :, at_g], cat_v[s, :, at_g]
        peak, total, out = softmax_parts(heads_of(queries, s, g), k, v, biases[0])
        put_heads(text_ref, (s,), g, out)
        t_own_stat[s, g] = pack_stats(peak, total, rows)
        peak, total, out = softmax_parts(heads_of(q_pair, s, g), k, v, biases[1])
        out = out * (1.0 / jnp.where(total > 0.0, total, 1.0))
        put_heads(t_send, (s,), g, out.astype(jnp.bfloat16))
        t_stat_send[s, g] = pack_stats(peak, total, rows)
        return carry

    lax.fori_loop(0, seqs * groups, text_step, 0)
    text_back = (send(t_send, t_recv, pair), send(t_stat_send, t_stat_recv, pair))

    image_diag = {}

    def forward(j):
        for k in range(1, members):
            s, d = slot_of("far", k), slot_of("diag", k)
            pieces = image_far[k, j]
            pieces[0].wait_recv()
            first = send(far_ik.at[s, j], far_ik.at[d, j], side)
            pieces[1].wait_recv()
            image_diag[k, j] = (first, send(far_iv.at[s, j], far_iv.at[d, j], side))

    def attend_far(slot, j):
        attend(far_ik.at[slot, j], far_iv.at[slot, j], (slot + 1) * here + j, (1, 0))

    for j in range(here):
        for piece in image_side[j]:
            piece.wait_recv()
        attend_far(0, j)
    for j in range(here):
        forward(j)
        for k in range(1, members):
            attend_far(slot_of("far", k), j)
        for k in range(1, members):
            for piece in image_diag[k, j]:
                piece.wait_recv()
            attend_far(slot_of("diag", k), j)

    row_pos = lax.broadcasted_iota(jnp.int32, (rows, LANES), 0)

    def visual_weights(s, g, which):
        seen, packed = [], []
        for j in range(per_seq):
            seen.append(thresholds[s * per_seq + j] <= row_pos + places[which])
            packed.append(stat[at[s * per_seq + j], which, g])
        peaks = [jnp.where(a, p, NEG) for a, p in zip(seen, packed)]
        overall = functools.reduce(jnp.maximum, peaks)
        weights = [jnp.where(a, jnp.exp(p - overall), 0.0) for a, p in zip(seen, peaks)]
        total = sum(w * totals_of(p) for w, p in zip(weights, packed))
        return overall, total, weights

    def weighted(s, g, which, h, weights):
        start = pl.multiple_of(g * (GROUP * DH), DH)
        return sum(
            w[:, h:h + 1] * num[at[s * per_seq + j], which, :, pl.ds(start + h * DH, DH)]
            for j, w in enumerate(weights)
        )

    def stat_lanes(overall, total):
        lane_id = lax.broadcasted_iota(jnp.int32, (rows, LANES), 1)
        return jnp.where(lane_id < HALF, overall, pltpu.roll(total, HALF, 1))

    visual_back = []
    for s in range(seqs):
        def pair_step(g, carry, s=s):
            overall, total, weights = visual_weights(s, g, 1)
            inverse = 1.0 / jnp.where(total > 0.0, total, 1.0)
            weights = [w * inverse for w in weights]
            start = pl.multiple_of(g * (GROUP * DH), DH)
            for h in range(GROUP):
                v_send[s, :, pl.ds(start + h * DH, DH)] = weighted(s, g, 1, h, weights).astype(
                    jnp.bfloat16
                )
            v_stat_send[s, g] = stat_lanes(overall, total)
            return carry

        lax.fori_loop(0, groups, pair_step, 0)
        visual_back.append((
            send(v_send.at[s], v_recv.at[s], pair), send(v_stat_send.at[s], v_stat_recv.at[s], pair)
        ))

    for piece in text_back:
        piece.wait_recv()

    def text_merge(i, carry):
        s, g = i // groups, i % groups
        ours, theirs = t_own_stat[s, g], t_stat_recv[s, g]
        overall = jnp.maximum(ours, theirs)
        weight_a = jnp.exp(ours - overall)
        weight_b = jnp.exp(theirs - overall) * totals_of(theirs)
        inverse = 1.0 / (weight_a * totals_of(ours) + weight_b)
        weight_a, weight_b = weight_a * inverse, weight_b * inverse
        start = pl.multiple_of(g * (GROUP * DH), DH)
        for h in range(GROUP):
            cut = pl.ds(start + h * DH, DH)
            text_ref[s, :, cut] = weight_a[:, h:h + 1] * text_ref[s, :, cut] + weight_b[
                :, h:h + 1
            ] * t_recv[s, :, cut].astype(jnp.float32)
        return carry

    lax.fori_loop(0, seqs * groups, text_merge, 0)

    for s in range(seqs):
        for piece in visual_back[s]:
            piece.wait_recv()

        def own_step(g, carry, s=s):
            overall, total, weights = visual_weights(s, g, 0)
            theirs = v_stat_recv[s, g]
            joint = jnp.maximum(overall, theirs)
            weight_a = jnp.exp(overall - joint)
            weight_b = jnp.exp(theirs - joint) * totals_of(theirs)
            inverse = 1.0 / (weight_a * total + weight_b)
            weights = [w * (weight_a * inverse) for w in weights]
            weight_b = weight_b * inverse
            start = pl.multiple_of(g * (GROUP * DH), DH)
            for h in range(GROUP):
                cut = pl.ds(start + h * DH, DH)
                visual_ref[s, :, cut] = weighted(s, g, 0, h, weights) + weight_b[
                    :, h:h + 1
                ] * v_recv[s, :, cut].astype(jnp.float32)
            return carry

        lax.fori_loop(0, groups, own_step, 0)

    for copy in copies:
        copy.wait_send()


def mix_kernel(gate_ref, text_ref, visual_ref, out_ref):
    gate = gate_ref[0]
    for h in range(gate.shape[-1]):
        cut = slice(h * DH, (h + 1) * DH)
        g = gate[:, h:h + 1]
        out_ref[0, :, cut] = ((1.0 - g) * text_ref[0, :, cut] + g * visual_ref[0, :, cut]).astype(
            jnp.bfloat16
        )


def on_device(n, heads_split, queries, text_keys, text_values, visual_keys, visual_values,
              gate_weight, text_offsets, image_sequence, image_position):
    seqs, rows, columns = queries.shape
    groups = text_keys.shape[-1] // DH
    here, tokens, kv_columns = visual_keys.shape
    me = lax.axis_index("seq")
    members, blocks = n // 4, n // 2

    partial_gate = jnp.dot(
        queries.reshape(seqs * rows, columns).astype(jnp.float32),
        gate_weight,
        precision=lax.Precision.HIGHEST,
    ).reshape(seqs, rows, heads_split, groups * GROUP)
    core = lax.axis_index("kvh")

    def share(k):
        return lax.dynamic_index_in_dim(partial_gate, (core + k) % heads_split, 2, keepdims=False)

    logits = share(0)
    for k in range(1, heads_split):
        logits = logits + lax.ppermute(
            share(k), "kvh", [(c, (c + k) % heads_split) for c in range(heads_split)]
        )
    gate = jax.nn.sigmoid(logits)

    far_ids = [(me // 4 + members - k) % members * 4 + me % 4 for k in range(1, members)]
    sources = jnp.stack([me, me ^ 1] + far_ids + [f ^ 1 for f in far_ids])
    image_ids = (sources[:, None] * here + jnp.arange(here, dtype=jnp.int32)).reshape(-1)
    owners = image_sequence[image_ids]
    slots = blocks * here
    per_seq = image_sequence.shape[0] // seqs
    mine = owners[None, :] == jnp.arange(seqs, dtype=jnp.int32)[:, None]
    rank = jnp.cumsum(mine.astype(jnp.int32), axis=1) - 1
    pick = mine[:, None, :] & (rank[:, None, :] == jnp.arange(per_seq, dtype=jnp.int32)[None, :, None])
    at = jnp.sum(jnp.where(pick, jnp.arange(slots, dtype=jnp.int32), 0), axis=-1).reshape(-1)
    thresholds = jnp.sum(jnp.where(pick, image_position[image_ids], 0), axis=-1)
    thresholds = jnp.where(jnp.any(pick, axis=-1), thresholds, FAR).reshape(-1)
    places = text_offsets[jnp.concatenate([jnp.stack([me, me ^ 2]), sources])]

    smem = pl.BlockSpec(memory_space=pltpu.SMEM)
    vmem = pl.BlockSpec(memory_space=pltpu.VMEM)
    bf16, f32 = jnp.bfloat16, jnp.float32
    count = 1 + 4 * (members - 1) + 2 + here * (4 * (members - 1) + 2) + 2 + 2 * seqs
    stats = (seqs, groups, rows, LANES)
    pairs = 2 * rows * GROUP * groups * (slots * tokens + seqs * blocks * rows)
    text, visual = pl.pallas_call(
        functools.partial(attention_kernel, n, seqs, rows, groups, here, per_seq),
        in_specs=[smem] * 4 + [vmem] * 5,
        out_specs=[vmem, vmem],
        out_shape=[jax.ShapeDtypeStruct(queries.shape, f32)] * 2,
        scratch_shapes=[
            pltpu.VMEM(queries.shape, bf16),
            pltpu.VMEM((blocks - 1, *text_keys.shape), bf16),
            pltpu.VMEM((blocks - 1, *text_keys.shape), bf16),
            pltpu.VMEM((blocks - 1, *visual_keys.shape), bf16),
            pltpu.VMEM((blocks - 1, *visual_keys.shape), bf16),
            pltpu.VMEM((slots, 2, rows, columns), f32),
            pltpu.VMEM((slots, 2, groups, rows, LANES), f32),
            pltpu.VMEM((seqs, blocks * rows, kv_columns), bf16),
            pltpu.VMEM((seqs, blocks * rows, kv_columns), bf16),
            pltpu.VMEM(queries.shape, bf16),
            pltpu.VMEM(stats, f32),
            pltpu.VMEM(queries.shape, bf16),
            pltpu.VMEM(stats, f32),
            pltpu.VMEM(queries.shape, bf16),
            pltpu.VMEM(stats, f32),
            pltpu.VMEM(queries.shape, bf16),
            pltpu.VMEM(stats, f32),
            pltpu.VMEM(stats, f32),
            pltpu.SemaphoreType.DMA((count,)),
            pltpu.SemaphoreType.DMA((count,)),
        ],
        compiler_params=pltpu.CompilerParams(
            collective_id=0, has_side_effects=True, vmem_limit_bytes=60 << 20
        ),
        cost_estimate=pl.CostEstimate(
            flops=4 * pairs * DH, bytes_accessed=16 << 20, transcendentals=pairs
        ),
    )(owners, places, at, thresholds, queries, text_keys, text_values, visual_keys, visual_values)

    wide = pl.BlockSpec((1, rows, columns), lambda s: (s, 0, 0))
    return pl.pallas_call(
        mix_kernel,
        grid=(seqs,),
        in_specs=[pl.BlockSpec((1, rows, groups * GROUP), lambda s: (s, 0, 0)), wide, wide],
        out_specs=wide,
        out_shape=jax.ShapeDtypeStruct(queries.shape, bf16),
    )(gate, text, visual)


def solution(mesh):
    return jax.shard_map(
        functools.partial(on_device, mesh.shape["seq"], mesh.shape["kvh"]),
        mesh=mesh,
        in_specs=(
            P("batch", "seq", "kvh"),
            P("batch", "seq", "kvh"),
            P("batch", "seq", "kvh"),
            P(("batch", "seq"), None, "kvh"),
            P(("batch", "seq"), None, "kvh"),
            P("kvh", None),
            P("batch"),
            P("batch"),
            P("batch"),
        ),
        out_specs=P("batch", "seq", "kvh"),
        check_vma=False,
    )
```

time: 374 us -> 150 us (0.40)
  waiting for transfers between devices: 210 us -> 0.01 us
  Pallas kernels: 0 us -> 137 us
  local copies, waits for them, and re-layouts: 67.9 us -> 7.17 us
  matrix products: 44 us -> 2.57 us
  other arithmetic: 32 us -> 1.47 us
  between operations: 14 us -> 0.11 us
  blocking collectives: 3.9 us -> 0 us
    all_gather x4 -> x0, waiting for transfers between devices: 209 us -> none  [the longest x1 72.3 us: on_device(): lax.all_gather(visual_values, 'seq', axis=0, tiled=True)]
    pallas_call x0 -> x2, Pallas kernels: none -> 137 us  [the longest x1 133 us: on_device(): pl.pallas_call(functools.partial(attention_kernel, n, seqs, rows, groups,...]
    dot_general x17 -> x1, matrix products: 44 us -> 2.57 us  [on_device(): jnp.dot(queries.reshape(seqs * rows, columns).astype(jnp.float32), gate_w...]
    gather x6 -> x3, local copies, waits for them, and re-layouts: 30.4 us -> 2.47 us  [the longest x1 1.19 us: on_device(): places = text_offsets[jnp.concatenate([jnp.stack([me, me ^ 2]), sources])]]
    reduce_sum x16 -> x1, other arithmetic: 22.8 us -> 0.22 us  [on_device(): thresholds = jnp.sum(jnp.where(pick, image_position[image_ids], 0), axis=-1)]
    unnamed x22 -> x14, local copies, waits for them, and re-layouts: 22.2 us -> 1.96 us
    reshape x6 -> x1, local copies, waits for them, and re-layouts: 7.29 us -> 0.6 us  [on_device(): jnp.sum(jnp.where(pick, jnp.arange(slots, dtype=jnp.int32), 0), axis=-1)]
    dynamic_slice x5 -> x3, local copies, waits for them, and re-layouts: 6.37 us -> 0.24 us  [share(): lax.dynamic_index_in_dim(partial_gate, (core + k) % heads_split, 2, keepd...]
  transfers between devices with their start and end apart: 4 -> 1, of which waited for: 4 -> 0; matrix products, arithmetic and copies ran while one was open for 17% -> 5% of each run, Pallas kernels for 0% -> 89%
where the time goes in v1:
time: 150 us; the launch traced here: 149 us
  Pallas kernels  137 us (91%)
  local copies, waits for them, and re-layouts  7.17 us (5%)
  matrix products  2.57 us (2%)
    pallas_call x1, Pallas kernels, on_device(): pl.pallas_call(functools.partial(attention_kernel, n, seqs, rows, groups,...  133 us
    pallas_call x1, Pallas kernels, on_device(): pl.pallas_call(mix_kernel, grid=(seqs,), in_specs=[pl.BlockSpec((1, rows,...  4.44 us
  transfers between devices with their start and end apart: 1, of which 0 were waited for; matrix products, arithmetic and copies ran while one was open for 5% of the time, Pallas kernels for 89%

profile of v1, /device:TPU:0, one launch (start us, length us, event | category | flops | bytes accessed | tf_op | source)
XLA Modules:
  0.0 149.3 jit_solution(9398272430687292659)
XLA Ops:
  0.0 0.0 copy-start
  0.0 1.0 reshape.377
  1.1 0.0 copy-start.4
  1.1 2.6 %fusion = f32[4,64,2,14]{1,3,2,0:T(8,128)S(1)} fusion(f32[2,14,1792,1]{2,1,0,3:T(8,128)S(1)} %reshape.377, bf16[4,64,1792]{2,1,0:T(8,128)(2,1)} %queries.1), kind=kOutput, calls=%fused_computation.3 | convolution fusion | flops 154140672 | bytes 1146880 | tf_op jit(solution)/shard_map/dot_general | solution.py:323
  3.7 0.1 copy.19
  3.8 0.6 collective-permute-start
  4.4 0.1 add_multiply_fusion
  4.4 0.1 iota_add_fusion
  4.5 0.1 add.100
  4.6 0.0 copy-done
  4.6 0.6 gather_fusion
  5.3 0.0 copy-start.2
  5.3 0.2 reduce_window_sum.11
  5.5 0.0 copy-done.1
  5.5 0.6 gather_fusion.2
  6.1 0.2 fusion.10
  6.3 0.2 select_reduce_fusion
  6.5 0.7 select_n.78.thresholds
  7.2 0.6 reshape.351.at
  7.8 0.1 concatenate.42
  7.9 0.0 copy-done.3
  7.9 1.0 copy.20.visual_keys
  8.9 0.0 copy-done.4
  8.9 1.0 copy.21.visual_values
  9.9 0.0 copy-done.2
  9.9 1.2 gather_fusion.1
  11.1 0.0 copy-done.5
  11.1 133.0 %shard_map.91 = (f32[4,64,1792]{2,1,0:T(8,128)}, f32[4,64,1792]{2,1,0:T(8,128)}) custom-call(s32[8]{0:T(128)} %copy-done.5, s32[6]{0:T(128)} %gather_fusion.1, s32[16]{0:T(128)} %reshape.351.at, s32[16]{0:T(128)} %select_n.78.thresholds, bf16[4,64,1792]{2,1,0:T(8,128)(2,1)} %queries.1, bf16[4,64,256]{2,1,0:T(8,128)(2,1)} %text_keys.1, ...), custom_call_target="tpu_custom_call" | custom-call | flops 6290407424 | bytes 16777216 | tf_op jit(solution)/shard_map/pallas_call | solution.py:360
  144.0 0.1 copy.18
  144.1 0.0 collective-permute-done
  144.2 0.7 fusion.5.gate_ref
  144.9 4.4 %shard_map.92 = bf16[4,64,1792]{2,1,0:T(8,128)(2,1)} custom-call(f32[4,64,14]{2,1,0:T(8,128)} %fusion.5.gate_ref, f32[4,64,1792]{2,1,0:T(8,128)} %get-tuple-element.7.text_ref, f32[4,64,1792]{2,1,0:T(8,128)} %get-tuple-element.8.visual_ref), custom_call_target="tpu_custom_call" | custom-call | tf_op jit(solution)/shard_map/pallas_call | solution.py:396
  (11 shorter events, 0.1 us)
Async XLA Ops:
  0.0 4.6 %copy-start = (s32[16]{0:T(128)S(1)}, s32[16]{0:T(128)}, u32[]{:S(2)}) copy-start(s32[16]{0:T(128)} %param.16) | copy-start | bytes 196
  0.0 5.5 %copy-start.1 = (s32[16]{0:T(128)S(1)}, s32[16]{0:T(128)}, u32[]{:S(2)}) copy-start(s32[16]{0:T(128)} %param.17) | copy-start | bytes 196
  0.0 7.9 %copy-start.3 = (bf16[2,729,256]{2,0,1:T(2,128)(2,1)S(1)}, bf16[2,729,256]{2,0,1:T(2,128)(2,1)}, u32[]{:S(2)}) copy-start(bf16[2,729,256]{2,0,1:T(2,128)(2,1)} %param.12) | copy-start | bytes 2239492
  1.1 7.9 %copy-start.4 = (bf16[2,729,256]{2,0,1:T(2,128)(2,1)S(1)}, bf16[2,729,256]{2,0,1:T(2,128)(2,1)}, u32[]{:S(2)}) copy-start(bf16[2,729,256]{2,0,1:T(2,128)(2,1)} %param.13) | copy-start | bytes 2239492
  3.8 140.4 %collective-permute-start = (f32[4,64,14]{2,1,0:T(8,128)S(1)}, f32[4,64,14]{2,1,0:T(8,128)S(1)}, u32[]{:S(2)}, u32[]{:S(2)}) collective-permute-start(f32[4,64,14]{2,1,0:T(8,128)S(1)} %bitcast.32), channel_id=1, source_target_pairs={{0,2},{2,0},{1,3},{3,1},{4,6},{6,4},{5,7},{7,5},{8,10},{10,8},{9,1... | collective-permute-start | bytes 43016 | tf_op jit(solution)/shard_map/ppermute | solution.py:335
  5.3 5.8 %copy-start.5 = (s32[8]{0:T(128)}, s32[8]{0:T(128)S(1)}, u32[]{:S(2)}) copy-start(s32[8]{0:T(128)S(1)} %gather_fusion) | copy-start | bytes 100
  5.3 4.6 %copy-start.2 = (s32[8]{0:T(128)S(1)}, s32[8]{0:T(128)}, u32[]{:S(2)}) copy-start(s32[8]{0:T(128)} %param.15) | copy-start | bytes 100

commit v2 on v1

--- a/solution.py
+++ b/solution.py
@@ -62,37 +62,64 @@
 
 
 def attention_kernel(
-    n, seqs, rows, groups, here, per_seq,
-    owners, places, at, thresholds,
-    queries, text_keys, text_values, visual_keys, visual_values,
-    text_ref, visual_ref,
+    n, heads_split, seqs, rows, groups, here, per_seq,
+    offsets, image_sequence, image_position,
+    queries, text_keys, text_values, visual_keys, visual_values, gate_weight,
+    out_ref,
     q_pair, far_tk, far_tv, far_ik, far_iv, num, stat, cat_k, cat_v,
     t_send, t_stat_send, t_recv, t_stat_recv, v_send, v_stat_send, v_recv, v_stat_recv,
-    t_own_stat, send_sems, recv_sems,
+    t_own, t_own_stat, gate_own, gate_recv, gate_buf, send_sems, recv_sems,
 ):
     me = lax.axis_index("seq")
+    core = lax.axis_index("kvh")
     members = n // 4
     blocks = n // 2
     pair = me // 4 * 4 + (me + 2) % 4
     side = me // 2 * 2 + (me + 1) % 2
     others = [(me // 4 + k) % members * 4 + me % 4 for k in range(1, members)]
+    twins = [(core + k) % heads_split for k in range(1, heads_split)]
+
+    far_ids = [(me // 4 + members - k) % members * 4 + me % 4 for k in range(1, members)]
+    sources = [me, side] + far_ids + [f // 2 * 2 + (f + 1) % 2 for f in far_ids]
+    places = [offsets[i] for i in (me, pair, *sources)]
+    image_ids = [source * here + j for source in sources for j in range(here)]
+    owners = [image_sequence[i] for i in image_ids]
+    positions = [image_position[i] for i in image_ids]
+    at, thresholds = [], []
+    for s in range(seqs):
+        slot_here = [jnp.int32(0)] * per_seq
+        threshold_here = [jnp.int32(FAR)] * per_seq
+        found = jnp.int32(0)
+        for slot, (owner, position) in enumerate(zip(owners, positions)):
+            hit = owner == s
+            for j in range(per_seq):
+                take = hit & (found == j)
+                slot_here[j] = jnp.where(take, slot, slot_here[j])
+                threshold_here[j] = jnp.where(take, position, threshold_here[j])
+            found = found + jnp.where(hit, 1, 0)
+        at += slot_here
+        thresholds += threshold_here
 
     barrier = pltpu.get_barrier_semaphore()
     for peer in (pair, side, *others):
         pl.semaphore_signal(
             barrier, inc=1, device_id={"seq": peer}, device_id_type=pl.DeviceIdType.MESH
         )
-    pl.semaphore_wait(barrier, 2 + len(others))
+    for twin in twins:
+        pl.semaphore_signal(
+            barrier, inc=1, device_id={"kvh": twin}, device_id_type=pl.DeviceIdType.MESH
+        )
+    pl.semaphore_wait(barrier, 2 + len(others) + len(twins))
 
     copies = []
 
-    def send(src, dst, peer):
+    def send(src, dst, peer, axis="seq"):
         copy = pltpu.make_async_remote_copy(
             src_ref=src,
             dst_ref=dst,
             send_sem=send_sems.at[len(copies)],
             recv_sem=recv_sems.at[len(copies)],
-            device_id={"seq": peer},
+            device_id={axis: peer},
             device_id_type=pl.DeviceIdType.MESH,
         )
         copy.start()
@@ -137,8 +164,20 @@
 
         lax.fori_loop(0, groups, step, 0)
 
+    rest = gate_weight[...]
+    q_all = queries[...].reshape(seqs * rows, queries.shape[-1])
+    logits = 0.0
+    for _ in range(3):
+        term = rest.astype(jnp.bfloat16)
+        rest = rest - term.astype(jnp.float32)
+        logits = logits + jnp.dot(q_all, term, preferred_element_type=jnp.float32)
+    gate_own[...] = logits.reshape(gate_own.shape)
+    t_stat_send[...] = jnp.zeros_like(t_stat_send)
+    v_stat_send[...] = jnp.zeros_like(v_stat_send)
+
     for j in range(here):
         attend(visual_keys.at[j], visual_values.at[j], j, (0,))
+    gates = [send(gate_own, gate_recv.at[k], twin, "kvh") for k, twin in enumerate(twins)]
 
     text_diag = []
     for k, pieces in enumerate(text_far, 1):
@@ -173,12 +212,12 @@
         at_g = pl.ds(pl.multiple_of(g * DH, DH), DH)
         k, v = cat_k[s, :, at_g], cat_v[s, :, at_g]
         peak, total, out = softmax_parts(heads_of(queries, s, g), k, v, biases[0])
-        put_heads(text_ref, (s,), g, out)
+        put_heads(t_own, (s,), g, out)
         t_own_stat[s, g] = pack_stats(peak, total, rows)
         peak, total, out = softmax_parts(heads_of(q_pair, s, g), k, v, biases[1])
         out = out * (1.0 / jnp.where(total > 0.0, total, 1.0))
         put_heads(t_send, (s,), g, out.astype(jnp.bfloat16))
-        t_stat_send[s, g] = pack_stats(peak, total, rows)
+        t_stat_send[s] = t_stat_send[s] + pltpu.roll(pack_stats(peak, total, rows), g * 8, 1)
         return carry
 
     lax.fori_loop(0, seqs * groups, text_step, 0)
@@ -195,8 +234,8 @@
             pieces[1].wait_recv()
             image_diag[k, j] = (first, send(far_iv.at[s, j], far_iv.at[d, j], side))
 
-    def attend_far(slot, j):
-        attend(far_ik.at[slot, j], far_iv.at[slot, j], (slot + 1) * here + j, (1, 0))
+    def attend_far(slot, j, sides=(1, 0)):
+        attend(far_ik.at[slot, j], far_iv.at[slot, j], (slot + 1) * here + j, sides)
 
     for j in range(here):
         for piece in image_side[j]:
@@ -209,7 +248,8 @@
         for k in range(1, members):
             for piece in image_diag[k, j]:
                 piece.wait_recv()
-            attend_far(slot_of("diag", k), j)
+            last = j == here - 1 and k == members - 1
+            attend_far(slot_of("diag", k), j, (1,) if last else (1, 0))
 
     row_pos = lax.broadcasted_iota(jnp.int32, (rows, LANES), 0)
 
@@ -233,7 +273,8 @@
 
     def stat_lanes(overall, total):
         lane_id = lax.broadcasted_iota(jnp.int32, (rows, LANES), 1)
-        return jnp.where(lane_id < HALF, overall, pltpu.roll(total, HALF, 1))
+        packed = jnp.where(lane_id < HALF, overall, pltpu.roll(total, HALF, 1))
+        return jnp.where(lane_id % HALF < GROUP, packed, 0.0)
 
     visual_back = []
     for s in range(seqs):
@@ -246,7 +287,7 @@
                 v_send[s, :, pl.ds(start + h * DH, DH)] = weighted(s, g, 1, h, weights).astype(
                     jnp.bfloat16
                 )
-            v_stat_send[s, g] = stat_lanes(overall, total)
+            v_stat_send[s] = v_stat_send[s] + pltpu.roll(stat_lanes(overall, total), g * 8, 1)
             return carry
 
         lax.fori_loop(0, groups, pair_step, 0)
@@ -254,12 +295,31 @@
             send(v_send.at[s], v_recv.at[s], pair), send(v_stat_send.at[s], v_stat_recv.at[s], pair)
         ))
 
+    attend_far(slot_of("diag", members - 1), here - 1, (0,))
+
+    for piece in gates:
+        piece.wait_recv()
+    for s in range(seqs):
+        logits = gate_own[s]
+        for k in range(len(twins)):
+            logits = logits + gate_recv[k, s]
+        heads = groups * GROUP
+        mine = logits[:, :heads]
+        for c in range(1, heads_split):
+            mine = jnp.where(core == c, logits[:, c * heads:(c + 1) * heads], mine)
+        mine = jax.nn.sigmoid(mine)
+        for g in range(groups):
+            gate_buf[s, g, :, :GROUP] = mine[:, g * GROUP:(g + 1) * GROUP]
+
     for piece in text_back:
         piece.wait_recv()
 
+    def unpacked(packed, g):
+        return pltpu.roll(packed, LANES - g * 8, 1)
+
     def text_merge(i, carry):
         s, g = i // groups, i % groups
-        ours, theirs = t_own_stat[s, g], t_stat_recv[s, g]
+        ours, theirs = t_own_stat[s, g], unpacked(t_stat_recv[s], g)
         overall = jnp.maximum(ours, theirs)
         weight_a = jnp.exp(ours - overall)
         weight_b = jnp.exp(theirs - overall) * totals_of(theirs)
@@ -268,7 +328,7 @@
         start = pl.multiple_of(g * (GROUP * DH), DH)
         for h in range(GROUP):
             cut = pl.ds(start + h * DH, DH)
-            text_ref[s, :, cut] = weight_a[:, h:h + 1] * text_ref[s, :, cut] + weight_b[
+            t_own[s, :, cut] = weight_a[:, h:h + 1] * t_own[s, :, cut] + weight_b[
                 :, h:h + 1
             ] * t_recv[s, :, cut].astype(jnp.float32)
         return carry
@@ -281,7 +341,7 @@
 
         def own_step(g, carry, s=s):
             overall, total, weights = visual_weights(s, g, 0)
-            theirs = v_stat_recv[s, g]
+            theirs = unpacked(v_stat_recv[s], g)
             joint = jnp.maximum(overall, theirs)
             weight_a = jnp.exp(overall - joint)
             weight_b = jnp.exp(theirs - joint) * totals_of(theirs)
@@ -291,25 +351,19 @@
             start = pl.multiple_of(g * (GROUP * DH), DH)
             for h in range(GROUP):
                 cut = pl.ds(start + h * DH, DH)
-                visual_ref[s, :, cut] = weighted(s, g, 0, h, weights) + weight_b[
-                    :, h:h + 1
-                ] * v_recv[s, :, cut].astype(jnp.float32)
+                visual = weighted(s, g, 0, h, weights) + weight_b[:, h:h + 1] * v_recv[
+                    s, :, cut
+                ].astype(jnp.float32)
+                gate = gate_buf[s, g, :, h:h + 1]
+                out_ref[s, :, cut] = ((1.0 - gate) * t_own[s, :, cut] + gate * visual).astype(
+                    jnp.bfloat16
+                )
             return carry
 
         lax.fori_loop(0, groups, own_step, 0)
 
     for copy in copies:
         copy.wait_send()
-
-
-def mix_kernel(gate_ref, text_ref, visual_ref, out_ref):
-    gate = gate_ref[0]
-    for h in range(gate.shape[-1]):
-        cut = slice(h * DH, (h + 1) * DH)
-        g = gate[:, h:h + 1]
-        out_ref[0, :, cut] = ((1.0 - g) * text_ref[0, :, cut] + g * visual_ref[0, :, cut]).astype(
-            jnp.bfloat16
-        )
 
 
 def on_device(n, heads_split, queries, text_keys, text_values, visual_keys, visual_values,
@@ -317,51 +371,22 @@
     seqs, rows, columns = queries.shape
     groups = text_keys.shape[-1] // DH
     here, tokens, kv_columns = visual_keys.shape
-    me = lax.axis_index("seq")
     members, blocks = n // 4, n // 2
-
-    partial_gate = jnp.dot(
-        queries.reshape(seqs * rows, columns).astype(jnp.float32),
-        gate_weight,
-        precision=lax.Precision.HIGHEST,
-    ).reshape(seqs, rows, heads_split, groups * GROUP)
-    core = lax.axis_index("kvh")
-
-    def share(k):
-        return lax.dynamic_index_in_dim(partial_gate, (core + k) % heads_split, 2, keepdims=False)
-
-    logits = share(0)
-    for k in range(1, heads_split):
-        logits = logits + lax.ppermute(
-            share(k), "kvh", [(c, (c + k) % heads_split) for c in range(heads_split)]
-        )
-    gate = jax.nn.sigmoid(logits)
-
-    far_ids = [(me // 4 + members - k) % members * 4 + me % 4 for k in range(1, members)]
-    sources = jnp.stack([me, me ^ 1] + far_ids + [f ^ 1 for f in far_ids])
-    image_ids = (sources[:, None] * here + jnp.arange(here, dtype=jnp.int32)).reshape(-1)
-    owners = image_sequence[image_ids]
     slots = blocks * here
     per_seq = image_sequence.shape[0] // seqs
-    mine = owners[None, :] == jnp.arange(seqs, dtype=jnp.int32)[:, None]
-    rank = jnp.cumsum(mine.astype(jnp.int32), axis=1) - 1
-    pick = mine[:, None, :] & (rank[:, None, :] == jnp.arange(per_seq, dtype=jnp.int32)[None, :, None])
-    at = jnp.sum(jnp.where(pick, jnp.arange(slots, dtype=jnp.int32), 0), axis=-1).reshape(-1)
-    thresholds = jnp.sum(jnp.where(pick, image_position[image_ids], 0), axis=-1)
-    thresholds = jnp.where(jnp.any(pick, axis=-1), thresholds, FAR).reshape(-1)
-    places = text_offsets[jnp.concatenate([jnp.stack([me, me ^ 2]), sources])]
-
     smem = pl.BlockSpec(memory_space=pltpu.SMEM)
     vmem = pl.BlockSpec(memory_space=pltpu.VMEM)
     bf16, f32 = jnp.bfloat16, jnp.float32
-    count = 1 + 4 * (members - 1) + 2 + here * (4 * (members - 1) + 2) + 2 + 2 * seqs
+    count = 1 + 4 * (members - 1) + 2 + here * (4 * (members - 1) + 2) + 2 + 2 * seqs + heads_split - 1
     stats = (seqs, groups, rows, LANES)
+    sent_stats = (seqs, rows, LANES)
+    gate_shape = (seqs, rows, gate_weight.shape[-1])
     pairs = 2 * rows * GROUP * groups * (slots * tokens + seqs * blocks * rows)
-    text, visual = pl.pallas_call(
-        functools.partial(attention_kernel, n, seqs, rows, groups, here, per_seq),
-        in_specs=[smem] * 4 + [vmem] * 5,
-        out_specs=[vmem, vmem],
-        out_shape=[jax.ShapeDtypeStruct(queries.shape, f32)] * 2,
+    return pl.pallas_call(
+        functools.partial(attention_kernel, n, heads_split, seqs, rows, groups, here, per_seq),
+        in_specs=[smem] * 3 + [vmem] * 6,
+        out_specs=vmem,
+        out_shape=jax.ShapeDtypeStruct(queries.shape, bf16),
         scratch_shapes=[
             pltpu.VMEM(queries.shape, bf16),
             pltpu.VMEM((blocks - 1, *text_keys.shape), bf16),
@@ -373,13 +398,17 @@
             pltpu.VMEM((seqs, blocks * rows, kv_columns), bf16),
             pltpu.VMEM((seqs, blocks * rows, kv_columns), bf16),
             pltpu.VMEM(queries.shape, bf16),
+            pltpu.VMEM(sent_stats, f32),
+            pltpu.VMEM(queries.shape, bf16),
+            pltpu.VMEM(sent_stats, f32),
+            pltpu.VMEM(queries.shape, bf16),
+            pltpu.VMEM(sent_stats, f32),
+            pltpu.VMEM(queries.shape, bf16),
+            pltpu.VMEM(sent_stats, f32),
+            pltpu.VMEM(queries.shape, f32),
             pltpu.VMEM(stats, f32),
-            pltpu.VMEM(queries.shape, bf16),
-            pltpu.VMEM(stats, f32),
-            pltpu.VMEM(queries.shape, bf16),
-            pltpu.VMEM(stats, f32),
-            pltpu.VMEM(queries.shape, bf16),
-            pltpu.VMEM(stats, f32),
+            pltpu.VMEM(gate_shape, f32),
+            pltpu.VMEM((heads_split - 1, *gate_shape), f32),
             pltpu.VMEM(stats, f32),
             pltpu.SemaphoreType.DMA((count,)),
             pltpu.SemaphoreType.DMA((count,)),
@@ -390,16 +419,10 @@
         cost_estimate=pl.CostEstimate(
             flops=4 * pairs * DH, bytes_accessed=16 << 20, transcendentals=pairs
         ),
-    )(owners, places, at, thresholds, queries, text_keys, text_values, visual_keys, visual_values)
-
-    wide = pl.BlockSpec((1, rows, columns), lambda s: (s, 0, 0))
-    return pl.pallas_call(
-        mix_kernel,
-        grid=(seqs,),
-        in_specs=[pl.BlockSpec((1, rows, groups * GROUP), lambda s: (s, 0, 0)), wide, wide],
-        out_specs=wide,
-        out_shape=jax.ShapeDtypeStruct(queries.shape, bf16),
-    )(gate, text, visual)
+    )(
+        text_offsets, image_sequence, image_position,
+        queries, text_keys, text_values, visual_keys, visual_values, gate_weight,
+    )
 
 
 def solution(mesh):

time: 150 us -> 136 us (0.907)
  Pallas kernels: 137 us -> 128 us
  matrix products: 2.57 us -> 0 us
    pallas_call x2 -> x1, Pallas kernels: 137 us -> 128 us  [on_device(): pl.pallas_call(functools.partial(attention_kernel, n, heads_split, seqs,...]
    unnamed x14 -> x8, local copies, waits for them, and re-layouts: 1.96 us -> 6.59 us
    dot_general x1 -> x0, matrix products: 2.57 us -> none  [on_device(): jnp.dot(queries.reshape(seqs * rows, columns).astype(jnp.float32), gate_w...]
    gather x3 -> x0, local copies, waits for them, and re-layouts: 2.47 us -> none  [the longest x1 1.19 us: on_device(): places = text_offsets[jnp.concatenate([jnp.stack([me, me ^ 2]), sources])]]
  transfers between devices with their start and end apart: 1 -> 0, of which waited for: 0 -> 0; matrix products, arithmetic and copies ran while one was open for 5% -> 0% of each run, Pallas kernels for 89% -> 0%
where the time goes in v2:
time: 136 us; the launch traced here: 135 us
  Pallas kernels  128 us (94%)
  local copies, waits for them, and re-layouts  6.59 us (5%)
    pallas_call x1, Pallas kernels, on_device(): pl.pallas_call(functools.partial(attention_kernel, n, heads_split, seqs,...  128 us
    unnamed x8, local copies, waits for them, and re-layouts  6.59 us

profile of v2, /device:TPU:0, one launch (start us, length us, event | category | flops | bytes accessed | tf_op | source)
XLA Modules:
  0.0 135.0 jit_solution(17382329173596444872)
XLA Ops:
  0.0 0.0 copy-start
  0.0 2.2 %copy.10.visual_keys = bf16[2,729,256]{2,1,0:T(8,128)(2,1)} copy(bf16[2,729,256]{2,0,1:T(2,128)(2,1)} %param.12) | data formatting | bytes 1492992 | tf_op args[3]
  2.2 0.0 copy-done
  2.2 0.0 copy-start.1
  2.2 1.0 copy.11.visual_values
  3.2 0.0 copy-done.1
  3.2 1.3 copy.12.gate_weight
  4.4 128.4 %shard_map.91 = bf16[4,64,1792]{2,1,0:T(8,128)(2,1)} custom-call(s32[8]{0:T(128)} %offsets.1, s32[16]{0:T(128)} %image_sequence.1, s32[16]{0:T(128)} %image_position.1, bf16[4,64,1792]{2,1,0:T(8,128)(2,1)} %queries.1, bf16[4,64,256]{2,1,0:T(8,128)(2,1)} %text_keys.1, bf16[4,64,256]{2,1,0:T(8,128)(2,1)} %text_values.1, ...), custom_call_target="tpu_custom_call" | custom-call | flops 6290407424 | bytes 16777216 | tf_op jit(solution)/shard_map/pallas_call | solution.py:385
  132.8 2.2 %copy.14 = bf16[4,64,1792]{2,1,0:T(8,128)(2,1)} copy(bf16[4,64,1792]{2,1,0:T(8,128)(2,1)} %shard_map.91) | data formatting | bytes 1835008
Async XLA Ops:
  0.0 2.2 %copy-start = (bf16[2,729,256]{2,0,1:T(2,128)(2,1)S(1)}, bf16[2,729,256]{2,0,1:T(2,128)(2,1)}, u32[]{:S(2)}) copy-start(bf16[2,729,256]{2,0,1:T(2,128)(2,1)} %param.13) | copy-start | bytes 2239492
  2.2 1.0 copy-start.1

commit v3 on v2

--- a/solution.py
+++ b/solution.py
@@ -12,11 +12,18 @@
 GROUP = 7
 LANES = 128
 HALF = LANES // 2
+CHUNKS = 4
+TILE = 16
 NEG = -1e30
 FLOOR = -1e29
 FAR = 1 << 30
 SCALE = 1.0 / DH ** 0.5
 SCALE2 = SCALE * math.log2(math.e)
+
+
+def chunks_of(tokens):
+    size = -(-tokens // (CHUNKS * TILE)) * TILE
+    return [pl.ds(a, min(size, tokens - a)) for a in range(0, tokens, size)]
 
 
 def heads_of(ref, lead, g):
@@ -112,6 +119,7 @@
     pl.semaphore_wait(barrier, 2 + len(others) + len(twins))
 
     copies = []
+    chunks = chunks_of(visual_values.shape[1])
 
     def send(src, dst, peer, axis="seq"):
         copy = pltpu.make_async_remote_copy(
@@ -140,10 +148,9 @@
     for j in range(here):
         for k, peer in enumerate(others, 1):
             s = slot_of("far", k)
-            image_far[k, j] = (
-                send(visual_keys.at[j], far_ik.at[s, j], peer),
-                send(visual_values.at[j], far_iv.at[s, j], peer),
-            )
+            image_far[k, j] = [send(visual_keys.at[j], far_ik.at[s, j], peer)] + [
+                send(visual_values.at[j, cut], far_iv.at[s, j, cut], peer) for cut in chunks
+            ]
         image_side[j] = (
             send(visual_keys.at[j], far_ik.at[0, j], side),
             send(visual_values.at[j], far_iv.at[0, j], side),
@@ -170,7 +177,9 @@
     for _ in range(3):
         term = rest.astype(jnp.bfloat16)
         rest = rest - term.astype(jnp.float32)
-        logits = logits + jnp.dot(q_all, term, preferred_element_type=jnp.float32)
+        logits = logits + lax.dot_general(
+            q_all, term, (((1,), (1,)), ((), ())), preferred_element_type=jnp.float32
+        )
     gate_own[...] = logits.reshape(gate_own.shape)
     t_stat_send[...] = jnp.zeros_like(t_stat_send)
     v_stat_send[...] = jnp.zeros_like(v_stat_send)
@@ -230,9 +239,10 @@
             s, d = slot_of("far", k), slot_of("diag", k)
             pieces = image_far[k, j]
             pieces[0].wait_recv()
-            first = send(far_ik.at[s, j], far_ik.at[d, j], side)
-            pieces[1].wait_recv()
-            image_diag[k, j] = (first, send(far_iv.at[s, j], far_iv.at[d, j], side))
+            image_diag[k, j] = [send(far_ik.at[s, j], far_ik.at[d, j], side)]
+            for cut, piece in zip(chunks, pieces[1:]):
+                piece.wait_recv()
+                image_diag[k, j].append(send(far_iv.at[s, j, cut], far_iv.at[d, j, cut], side))
 
     def attend_far(slot, j, sides=(1, 0)):
         attend(far_ik.at[slot, j], far_iv.at[slot, j], (slot + 1) * here + j, sides)
@@ -377,7 +387,7 @@
     smem = pl.BlockSpec(memory_space=pltpu.SMEM)
     vmem = pl.BlockSpec(memory_space=pltpu.VMEM)
     bf16, f32 = jnp.bfloat16, jnp.float32
-    count = 1 + 4 * (members - 1) + 2 + here * (4 * (members - 1) + 2) + 2 + 2 * seqs + heads_split - 1
+    count = 1 + 4 * (members - 1) + 2 + here * (2 * (members - 1) * (1 + len(chunks_of(tokens))) + 2) + 2 + 2 * seqs + heads_split - 1
     stats = (seqs, groups, rows, LANES)
     sent_stats = (seqs, rows, LANES)
     gate_shape = (seqs, rows, gate_weight.shape[-1])
@@ -421,7 +431,7 @@
         ),
     )(
         text_offsets, image_sequence, image_position,
-        queries, text_keys, text_values, visual_keys, visual_values, gate_weight,
+        queries, text_keys, text_values, visual_keys, visual_values, gate_weight.T,
     )
 
 

time: 136 us -> 135 us (level)
    unnamed x8 -> x5, local copies, waits for them, and re-layouts: 6.59 us -> 5.31 us
where the time goes in v3:
time: 135 us; the launch traced here: 134 us
  Pallas kernels  128 us (95%)
  local copies, waits for them, and re-layouts  5.31 us (4%)
    pallas_call x1, Pallas kernels, on_device(): pl.pallas_call(functools.partial(attention_kernel, n, heads_split, seqs,...  128 us
    unnamed x5, local copies, waits for them, and re-layouts  5.31 us

profile of v3, /device:TPU:0, one launch (start us, length us, event | category | flops | bytes accessed | tf_op | source)
XLA Modules:
  0.0 133.7 jit_solution(13259375705533447291)
XLA Ops:
  0.0 0.0 copy-start
  0.0 2.2 %copy.10.visual_keys = bf16[2,729,256]{2,1,0:T(8,128)(2,1)} copy(bf16[2,729,256]{2,0,1:T(2,128)(2,1)} %param.12) | data formatting | bytes 1492992 | tf_op args[3]
  2.2 0.0 copy-done
  2.2 1.0 copy.11.visual_values
  3.1 128.3 %shard_map.91 = bf16[4,64,1792]{2,1,0:T(8,128)(2,1)} custom-call(s32[8]{0:T(128)} %offsets.1, s32[16]{0:T(128)} %image_sequence.1, s32[16]{0:T(128)} %image_position.1, bf16[4,64,1792]{2,1,0:T(8,128)(2,1)} %queries.1, bf16[4,64,256]{2,1,0:T(8,128)(2,1)} %text_keys.1, bf16[4,64,256]{2,1,0:T(8,128)(2,1)} %text_values.1, ...), custom_call_target="tpu_custom_call" | custom-call | flops 6290407424 | bytes 16777216 | tf_op jit(solution)/shard_map/pallas_call | solution.py:395
  131.5 2.2 %copy.13 = bf16[4,64,1792]{2,1,0:T(8,128)(2,1)} copy(bf16[4,64,1792]{2,1,0:T(8,128)(2,1)} %shard_map.91) | data formatting | bytes 1835008
Async XLA Ops:
  0.0 2.2 %copy-start = (bf16[2,729,256]{2,0,1:T(2,128)(2,1)S(1)}, bf16[2,729,256]{2,0,1:T(2,128)(2,1)}, u32[]{:S(2)}) copy-start(bf16[2,729,256]{2,0,1:T(2,128)(2,1)} %param.13) | copy-start | bytes 2239492
